TPU v7x, 128 devices: a whole 4x4x4 slice. The times are simulated.
128 devices in a mesh: gx: 8 (over x, core), gy: 4 (over z), band: 4 (over y).
Axes of the slice: x: 4, y: 4, z: 4, core: 2. Of those that a mesh axis runs over, the one named last changes fastest.
Arguments:
- block: float32 [32, 96, 18432], P('band', 'gx', 'gy'), may hold values from -9 to 9
- prior: float32 [256, 96, 18432], P('band', 'gx', 'gy'), may hold values from -9 to 9
- potential: float32 [96, 18432], P('gx', 'gy'), may hold values from -1.5 to 1
Outputs:
- orbitals: float32 [32, 96, 18432], P('band', 'gx', 'gy')
All inputs are finite; a program needn't handle non-finite values.
Results may differ from a plain program's by a relative error of at most 0.000098.
Values sent between devices are 32-bit elements; how exact they have to be, the bound alone decides.
A program may use at most 128 MiB of HBM per device.

v0:
```python
import jax
import jax.numpy as jnp
from jax import lax
from jax.sharding import PartitionSpec as P

NZ = 192
coeffs = (-205.0 / 72.0, 8.0 / 5.0, -1.0 / 5.0, 8.0 / 315.0, -1.0 / 560.0)


def extended_2(x, sides, width):
    for axis, dim in sides:
        devices, length = (lax.axis_size(axis), x.shape[dim])
        up = [(i, (i + 1) % devices) for i in range(devices - 1)]
        down = [(j, i) for i, j in up]
        last = lax.slice_in_dim(x, length - width, length, axis=dim)
        leading = lax.slice_in_dim(x, 0, width, axis=dim)
        before = lax.ppermute(last, axis, up)
        after = lax.ppermute(leading, axis, down)
        x = jnp.concatenate([before, x, after], axis=dim)
    return x


def laplace(padded):
    center = padded[:, 4:-4, 4:-4, 4:-4]
    total = 3.0 * coeffs[0] * center
    for shift in range(1, 5):
        total = total + coeffs[shift] * (
            padded[:, 4 + shift : padded.shape[1] - 4 + shift, 4:-4, 4:-4]
            + padded[:, 4 - shift : padded.shape[1] - 4 - shift, 4:-4, 4:-4]
        )
        total = total + coeffs[shift] * (
            padded[:, 4:-4, 4 + shift : padded.shape[2] - 4 + shift, 4:-4]
            + padded[:, 4:-4, 4 - shift : padded.shape[2] - 4 - shift, 4:-4]
        )
        total = total + coeffs[shift] * (
            padded[:, 4:-4, 4:-4, 4 + shift : padded.shape[3] - 4 + shift]
            + padded[:, 4:-4, 4:-4, 4 - shift : padded.shape[3] - 4 - shift]
        )
    return total


def matmul(left, right):
    return jnp.dot(left, right, precision=lax.Precision.HIGHEST, preferred_element_type=jnp.float32)


def shards(block, prior, potential):
    own_count = block.shape[0]
    rows_x = block.shape[1]
    rows_y = block.shape[2] // NZ
    total_count = own_count * lax.axis_size("band")
    ncells_all = rows_x * lax.axis_size("gx") * rows_y * lax.axis_size("gy") * NZ
    grid_block = block.reshape(own_count, rows_x, rows_y, NZ)
    extended = extended_2(grid_block, (("gx", 1), ("gy", 2)), 4)
    extended = jnp.pad(extended, ((0, 0), (0, 0), (0, 0), (4, 4)))
    lap_flat = laplace(extended).reshape(block.shape)
    phi = -2.0 * lap_flat + potential[None] * block
    phi_flat = phi.reshape(own_count, -1)
    prior_flat = prior.reshape(prior.shape[0], -1)
    phi_all = lax.all_gather(phi_flat, "band", axis=0, tiled=True)
    correlation = lax.psum(matmul(prior_flat, phi_all.T), ("gx", "gy")) / ncells_all
    removed = lax.psum_scatter(
        matmul(correlation.T, prior_flat), "band", scatter_dimension=0, tiled=True
    )
    projected_own = phi_flat - removed
    projected = lax.all_gather(projected_own, "band", axis=0, tiled=True)
    gram = lax.psum(matmul(projected, projected.T), ("gx", "gy")) / ncells_all
    lower = jnp.linalg.cholesky(gram)
    inverse = lax.linalg.triangular_solve(
        lower, jnp.eye(total_count, dtype=lower.dtype), left_side=True, lower=True
    )
    first_row = lax.axis_index("band") * own_count
    own_rows = lax.dynamic_slice_in_dim(inverse, first_row, own_count, 0)
    orbitals = matmul(own_rows, projected)
    return orbitals.reshape(block.shape)


def solution(mesh):
    in_specs = (P("band", "gx", "gy"), P("band", "gx", "gy"), P("gx", "gy"))
    out_specs = P("band", "gx", "gy")
    return jax.shard_map(shards, mesh=mesh, in_specs=in_specs, out_specs=out_specs, check_vma=False)
```

profile of v0, /device:TPU:0, one launch (start us, length us, event | category | flops | bytes accessed | tf_op | source)
XLA Modules:
  0.0 602.9 jit_solution(7956143481172874915)
XLA Ops:
  6.5 2.0 reshape.25
  8.7 1.3 collective-permute-start.1
  10.0 1.3 collective-permute-start
  12.9 3.1 collective-permute-done
  17.7 4.6 collective-permute-start.3
  22.3 6.6 %collective-permute-done.2 = f32[8,20,4,192]{3,2,0,1:T(4,128)S(1)} collective-permute-done((f32[8,20,4,192]{3,2,0,1:T(4,128)S(1)}, f32[8,20,4,192]{3,2,0,1:T(4,128)S(1)}, u32[]{:S(2)}, u32[]{:S(2)}) %collective-permute-start.2) | collective-permute-done | bytes 491552 | tf_op jit(solution)/shard_map/ppermute | solution.py:18
  28.9 1.5 collective-permute-done.3
  30.3 2.9 select_maximum_fusion
  33.2 20.7 %fusion.9 = f32[8,12,24,192]{3,2,0,1:T(8,128)} fusion(f32[8,20,24,192]{3,2,0,1:T(8,128)} %copy-done.3, f32[8,20,4,192]{3,2,0,1:T(4,128)S(1)} %collective-permute-done.3, f32[8,20,4,192]{3,2,0,1:T(4,128)S(1)} %collective-permute-done.2, f32[8,20,32,200]{3,2,0,1:T(8,128)S(1)} %select_maximum_fusion, f32[8,16,24,192]{3,2,0,1:T(8,128)} %copy-done.1, ...), kind=kLoop, calls=%fused_computation.25 | loop fusion | flops 20348928 | bytes 35782656 | tf_op jit(solution)/shard_map/mul | solution.py:56
  53.9 2.3 mul.78
  56.2 2.4 multiply_add_fusion
  58.9 11.4 %copy.10 = f32[12,8,8,4608]{3,2,0,1:T(8,128)} copy(f32[12,8,8,4608]{3,2,1,0:T(8,128)} %bitcast.31) | data formatting | bytes 28311552 | tf_op jit(solution)/shard_map/reshape | solution.py:58
  70.3 79.2 %all-gather.3.cloned.1.call-done = f32[32,55296]{1,0:T(8,128)} async-done(((f32[8,55296]{1,0:T(8,128)}), f32[32,55296]{1,0:T(8,128)}) %all-gather.3.cloned.1.call-update) | async-done | bytes 7077904 | tf_op jit(solution)/shard_map/all_gather | solution.py:59
  149.5 14.5 %convolution_bitcast_fusion = f32[64,32]{0,1:T(8,128)S(1)} fusion(f32[32,55296]{1,0:T(8,128)} %all-gather.3.cloned.1.call-done, f32[64,55296]{1,0:T(8,128)} %bitcast.27), kind=kOutput, calls=%fused_computation.63 | convolution fusion | flops 1358954496 | bytes 21241856 | tf_op jit(solution)/shard_map/dot_general | solution.py:43
  164.0 128.3 %psum.14 = f32[64,32]{0,1:T(8,128)S(1)} all-reduce(f32[64,32]{0,1:T(8,128)S(1)} %convolution_bitcast_fusion), channel_id=1, replica_groups=mesh['gx'=8,'gy'=4,'band'=4] {'gx','gy'}, use_global_device_ids=true, to_apply=%region_0.1 | all-reduce | flops 2048 | bytes 16384 | tf_op jit(solution)/shard_map/psum | solution.py:60
  292.3 11.7 %fusion.40 = f32[32,55296]{1,0:T(8,128)} fusion(f32[64,55296]{1,0:T(8,128)} %bitcast.28, f32[64,32]{0,1:T(8,128)S(1)} %psum.14), kind=kOutput, calls=%fused_computation.78 | convolution fusion | flops 1358956544 | bytes 21241856 | tf_op jit(solution)/shard_map/dot_general | solution.py:43
  304.0 66.2 %reduce-scatter.2.cloned.1.call-done = f32[8,55296]{1,0:T(8,128)} async-done(((f32[32,55296]{1,0:T(8,128)}), f32[8,55296]{1,0:T(8,128)}) %reduce-scatter.2.cloned.1.call-update) | async-done | bytes 1769488 | tf_op jit(solution)/shard_map/reduce_scatter | solution.py:61
  370.3 2.9 sub.3
  373.1 72.1 %all-gather.5.cloned.1.call-done = f32[32,55296]{1,0:T(8,128)} async-done(((f32[8,55296]{1,0:T(8,128)}), f32[32,55296]{1,0:T(8,128)}) %all-gather.5.cloned.1.call-update) | async-done | bytes 7077904 | tf_op jit(solution)/shard_map/all_gather | solution.py:65
  445.3 9.1 %fusion.49 = f32[32,32]{0,1:T(8,128)S(1)} fusion(f32[32,55296]{1,0:T(8,128)} %all-gather.5.cloned.1.call-done), kind=kOutput, calls=%fused_computation.91 | convolution fusion | flops 679477248 | bytes 7081984 | tf_op jit(solution)/shard_map/dot_general | solution.py:43
  454.4 128.5 %psum.15 = f32[32,32]{0,1:T(8,128)S(1)} all-reduce(f32[32,32]{0,1:T(8,128)S(1)} %fusion.49), channel_id=1, replica_groups=mesh['gx'=8,'gy'=4,'band'=4] {'gx','gy'}, use_global_device_ids=true, to_apply=%region_2.3 | all-reduce | flops 1024 | bytes 8192 | tf_op jit(solution)/shard_map/psum | solution.py:66
  583.0 2.9 cholesky.17
  587.2 2.4 custom-call.6
  589.9 6.5 %fusion.43 = f32[8,55296]{1,0:T(8,128)} fusion(f32[32,55296]{1,0:T(8,128)} %all-gather.5.cloned.1.call-done, f32[32,32]{1,0:T(8,128)S(1)} %fusion.37, s32[]{:T(128)S(6)} %select_n.8), kind=kOutput, calls=%fused_computation.84 | convolution fusion | flops 169869312 | bytes 8851460 | tf_op jit(solution)/shard_map/dot_general | solution.py:43
  (32 shorter events, 5.3 us)
Async XLA Ops:
  6.5 142.9 %all-gather.3.cloned.1.call-start = ((), (), s32[]{:S(2)}) async-start(), calls=%async_computation.1 | async-start | bytes 8847360 | tf_op jit(solution)/shard_map/all_gather | solution.py:59
  8.5 3.5 copy-start.2
  8.7 3.2 collective-permute-start.1
  10.0 5.9 collective-permute-start
  12.9 3.5 copy-start.1
  16.1 17.1 %copy-start = (f32[8,16,24,192]{3,2,0,1:T(8,128)}, f32[8,16,24,192]{3,2,0,1:T(8,128)S(1)}, u32[]{:S(2)}) copy-start(f32[8,16,24,192]{3,2,0,1:T(8,128)S(1)} %get-tuple-element.12) | copy-start | bytes 7077892
  16.1 17.1 %copy-start.3 = (f32[8,20,24,192]{3,2,0,1:T(8,128)}, f32[8,20,24,192]{3,2,0,1:T(8,128)S(1)}, u32[]{:S(2)}) copy-start(f32[8,20,24,192]{3,2,0,1:T(8,128)S(1)} %get-tuple-element.13) | copy-start | bytes 8847364
  16.4 12.5 %collective-permute-start.2 = (f32[8,20,4,192]{3,2,0,1:T(4,128)S(1)}, f32[8,20,4,192]{3,2,0,1:T(4,128)S(1)}, u32[]{:S(2)}, u32[]{:S(2)}) collective-permute-start(f32[8,20,4,192]{3,2,0,1:T(4,128)S(1)} %get-tuple-element.5), channel_id=1, source_target_pairs={{4,0},{8,4},{12,8},{5,1},{9,5},{13,9},{6,2},{10,6},{14,10},{7,3},{... | collective-permute-start | bytes 1474568 | tf_op jit(solution)/shard_map/ppermute | solution.py:18
  17.7 12.6 %collective-permute-start.3 = (f32[8,20,4,192]{3,2,0,1:T(4,128)S(1)}, f32[8,20,4,192]{3,2,0,1:T(4,128)S(1)}, u32[]{:S(2)}, u32[]{:S(2)}) collective-permute-start(f32[8,20,4,192]{3,2,0,1:T(4,128)S(1)} %get-tuple-element.6), channel_id=1, source_target_pairs={{0,4},{4,8},{8,12},{1,5},{5,9},{9,13},{2,6},{6,10},{10,14},{3,7},{... | collective-permute-start | bytes 1474568 | tf_op jit(solution)/shard_map/ppermute | solution.py:17
  53.9 2.3 copy-start.5
  58.7 311.6 %reduce-scatter.2.cloned.1.call-start = ((), (), s32[]{:S(2)}) async-start(), calls=%async_computation.2 | async-start | bytes 8847360 | tf_op jit(solution)/shard_map/reduce_scatter | solution.py:61
  304.0 66.3 %copy-start.4 = (f32[8,12,4608]{2,0,1:T(8,128)S(1)}, f32[8,12,4608]{2,0,1:T(8,128)}, u32[]{:S(2)}) copy-start(f32[8,12,4608]{2,0,1:T(8,128)} %multiply_add_fusion) | copy-start | bytes 5308420
  304.0 141.3 %all-gather.5.cloned.1.call-start = ((), (), s32[]{:S(2)}) async-start(), calls=%async_computation.3 | async-start | bytes 8847360 | tf_op jit(solution)/shard_map/all_gather | solution.py:65
Sparse Core Ops, SparseCore 0:
  58.8 90.6 all-gather.2
  304.1 66.1 reduce-scatter.1
  373.3 71.9 all-gather.4
where the time goes:
time: 603 us
  blocking collectives  257 us (43%)
  waiting for transfers between devices  229 us (38%)
  matrix products  42 us (7%)
  other arithmetic  35.5 us (6%)
  local copies, waits for them, and re-layouts  17.2 us (3%)
  between operations  13.3 us (2%)
  starting transfers between devices  8.78 us (1%)
    psum x1, blocking collectives, shards(): gram = lax.psum(matmul(projected, projected.T), ('gx', 'gy')) / ncells_all  129 us
    psum x1, blocking collectives, shards(): lax.psum(matmul(prior_flat, phi_all.T), ('gx', 'gy')) / ncells_all  128 us
    all_gather x1, waiting for transfers between devices, shards(): phi_all = lax.all_gather(phi_flat, 'band', axis=0, tiled=True)  79.2 us
    all_gather x1, waiting for transfers between devices, shards(): projected = lax.all_gather(projected_own, 'band', axis=0, tiled=True)  72.1 us
    reduce_scatter x1, waiting for transfers between devices, shards(): lax.psum_scatter(matmul(correlation.T, prior_flat), 'band', scatter_dimen...  66.2 us
    dot_general x4, matrix products, matmul(): jnp.dot(left, right, precision=lax.Precision.HIGHEST, preferred_element_t...  41.8 us
    mul x1, other arithmetic, shards(): phi = -2.0 * lap_flat + potential[None] * block  20.7 us
  transfers between devices with their start and end apart: 7, of which 7 were waited for; matrix products, arithmetic and copies ran while one was open for 2% of the time, Pallas kernels for 0%

commit v1 on v0

--- a/solution.py
+++ b/solution.py
@@ -63,7 +63,9 @@
     )
     projected_own = phi_flat - removed
     projected = lax.all_gather(projected_own, "band", axis=0, tiled=True)
-    gram = lax.psum(matmul(projected, projected.T), ("gx", "gy")) / ncells_all
+    gram = (
+        jnp.sum(lax.all_gather(matmul(projected, projected.T), ("gx", "gy")), axis=0) / ncells_all
+    )
     lower = jnp.linalg.cholesky(gram)
     inverse = lax.linalg.triangular_solve(
         lower, jnp.eye(total_count, dtype=lower.dtype), left_side=True, lower=True

time: 603 us -> 519 us (0.86)
  blocking collectives: 257 us -> 172 us
    psum x1 -> x0, blocking collectives: 129 us -> none  [shards(): gram = lax.psum(matmul(projected, projected.T), ('gx', 'gy')) / ncells_all]
    all_gather x0 -> x1, blocking collectives: none -> 44.1 us  [shards(): lax.all_gather(matmul(projected, projected.T), ('gx', 'gy'))]
where the time goes in v1:
time: 519 us; the launch traced here: 518 us
  waiting for transfers between devices  229 us (44%)
  blocking collectives  172 us (33%)
  matrix products  41.9 us (8%)
  other arithmetic  35.6 us (7%)
  local copies, waits for them, and re-layouts  17.3 us (3%)
  between operations  13.3 us (3%)
  starting transfers between devices  8.78 us (2%)
    psum x1, blocking collectives, shards(): lax.psum(matmul(prior_flat, phi_all.T), ('gx', 'gy')) / ncells_all  128 us
    all_gather x1, waiting for transfers between devices, shards(): phi_all = lax.all_gather(phi_flat, 'band', axis=0, tiled=True)  79.2 us
    all_gather x1, waiting for transfers between devices, shards(): projected = lax.all_gather(projected_own, 'band', axis=0, tiled=True)  72.1 us
    reduce_scatter x1, waiting for transfers between devices, shards(): lax.psum_scatter(matmul(correlation.T, prior_flat), 'band', scatter_dimen...  66.2 us
    all_gather x1, blocking collectives, shards(): lax.all_gather(matmul(projected, projected.T), ('gx', 'gy'))  44.1 us
    dot_general x4, matrix products, matmul(): jnp.dot(left, right, precision=lax.Precision.HIGHEST, preferred_element_t...  41.7 us
    mul x1, other arithmetic, shards(): phi = -2.0 * lap_flat + potential[None] * block  20.7 us
    reshape x1, local copies, waits for them, and re-layouts, shards(): prior_flat = prior.reshape(prior.shape[0], -1)  11.4 us
  transfers between devices with their start and end apart: 7, of which 7 were waited for; matrix products, arithmetic and copies ran while one was open for 2% of the time, Pallas kernels for 0%

profile of v1, /device:TPU:0, one launch (start us, length us, event | category | flops | bytes accessed | tf_op | source)
XLA Modules:
  0.0 518.5 jit_solution(16955316630726408968)
XLA Ops:
  6.5 2.0 reshape.25
  8.7 1.3 collective-permute-start.1
  10.0 1.3 collective-permute-start
  12.9 3.1 collective-permute-done
  17.7 4.6 collective-permute-start.3
  22.3 6.6 %collective-permute-done.2 = f32[8,20,4,192]{3,2,0,1:T(4,128)S(1)} collective-permute-done((f32[8,20,4,192]{3,2,0,1:T(4,128)S(1)}, f32[8,20,4,192]{3,2,0,1:T(4,128)S(1)}, u32[]{:S(2)}, u32[]{:S(2)}) %collective-permute-start.2) | collective-permute-done | bytes 491552 | tf_op jit(solution)/shard_map/ppermute | solution.py:18
  28.9 1.5 collective-permute-done.3
  30.3 2.9 select_maximum_fusion
  33.2 20.7 %fusion.9 = f32[8,12,24,192]{3,2,0,1:T(8,128)} fusion(f32[8,20,24,192]{3,2,0,1:T(8,128)} %copy-done.3, f32[8,20,4,192]{3,2,0,1:T(4,128)S(1)} %collective-permute-done.3, f32[8,20,4,192]{3,2,0,1:T(4,128)S(1)} %collective-permute-done.2, f32[8,20,32,200]{3,2,0,1:T(8,128)S(1)} %select_maximum_fusion, f32[8,16,24,192]{3,2,0,1:T(8,128)} %copy-done.1, ...), kind=kLoop, calls=%fused_computation.25 | loop fusion | flops 20348928 | bytes 35782656 | tf_op jit(solution)/shard_map/mul | solution.py:56
  53.9 2.3 mul.78
  56.2 2.4 multiply_add_fusion
  58.9 11.4 %copy.10 = f32[12,8,8,4608]{3,2,0,1:T(8,128)} copy(f32[12,8,8,4608]{3,2,1,0:T(8,128)} %bitcast.32) | data formatting | bytes 28311552 | tf_op jit(solution)/shard_map/reshape | solution.py:58
  70.3 79.2 %all-gather.4.cloned.1.call-done = f32[32,55296]{1,0:T(8,128)} async-done(((f32[8,55296]{1,0:T(8,128)}), f32[32,55296]{1,0:T(8,128)}) %all-gather.4.cloned.1.call-update) | async-done | bytes 7077904 | tf_op jit(solution)/shard_map/all_gather | solution.py:59
  149.5 14.5 %convolution_bitcast_fusion = f32[64,32]{0,1:T(8,128)S(1)} fusion(f32[32,55296]{1,0:T(8,128)} %all-gather.4.cloned.1.call-done, f32[64,55296]{1,0:T(8,128)} %bitcast.28), kind=kOutput, calls=%fused_computation.63 | convolution fusion | flops 1358954496 | bytes 21241856 | tf_op jit(solution)/shard_map/dot_general | solution.py:43
  164.0 128.3 %psum.7 = f32[64,32]{0,1:T(8,128)S(1)} all-reduce(f32[64,32]{0,1:T(8,128)S(1)} %convolution_bitcast_fusion), channel_id=1, replica_groups=mesh['gx'=8,'gy'=4,'band'=4] {'gx','gy'}, use_global_device_ids=true, to_apply=%region_0.1 | all-reduce | flops 2048 | bytes 16384 | tf_op jit(solution)/shard_map/psum | solution.py:60
  292.3 11.7 %fusion.40 = f32[32,55296]{1,0:T(8,128)} fusion(f32[64,55296]{1,0:T(8,128)} %bitcast.29, f32[64,32]{0,1:T(8,128)S(1)} %psum.7), kind=kOutput, calls=%fused_computation.78 | convolution fusion | flops 1358956544 | bytes 21241856 | tf_op jit(solution)/shard_map/dot_general | solution.py:43
  304.0 66.2 %reduce-scatter.2.cloned.1.call-done = f32[8,55296]{1,0:T(8,128)} async-done(((f32[32,55296]{1,0:T(8,128)}), f32[8,55296]{1,0:T(8,128)}) %reduce-scatter.2.cloned.1.call-update) | async-done | bytes 1769488 | tf_op jit(solution)/shard_map/reduce_scatter | solution.py:61
  370.3 2.9 sub.3
  373.1 72.1 %all-gather.6.cloned.1.call-done = f32[32,55296]{1,0:T(8,128)} async-done(((f32[8,55296]{1,0:T(8,128)}), f32[32,55296]{1,0:T(8,128)}) %all-gather.6.cloned.1.call-update) | async-done | bytes 7077904 | tf_op jit(solution)/shard_map/all_gather | solution.py:65
  445.3 9.0 %fusion.49 = f32[32,32]{1,0:T(8,128)S(1)} fusion(f32[32,55296]{1,0:T(8,128)} %all-gather.6.cloned.1.call-done), kind=kOutput, calls=%fused_computation.91 | convolution fusion | flops 679477248 | bytes 7081984 | tf_op jit(solution)/shard_map/dot_general | solution.py:43
  454.3 44.1 %all-gather = f32[1024,32]{1,0:T(8,128)S(1)} all-gather(f32[32,32]{1,0:T(8,128)S(1)} %fusion.49), channel_id=2, replica_groups=mesh['gx'=8,'gy'=4,'band'=4] {'gx','gy'}, dimensions={0}, use_global_device_ids=true | all-gather | bytes 135168 | tf_op jit(solution)/shard_map/all_gather | solution.py:67
  498.6 2.9 cholesky.17
  502.8 2.4 custom-call.6
  505.5 6.5 %fusion.43 = f32[8,55296]{1,0:T(8,128)} fusion(f32[32,55296]{1,0:T(8,128)} %all-gather.6.cloned.1.call-done, f32[32,32]{1,0:T(8,128)S(1)} %fusion.37, s32[]{:T(128)S(6)} %select_n.8), kind=kOutput, calls=%fused_computation.84 | convolution fusion | flops 169869312 | bytes 8851460 | tf_op jit(solution)/shard_map/dot_general | solution.py:43
  (34 shorter events, 5.4 us)
Async XLA Ops:
  6.5 142.9 %all-gather.4.cloned.1.call-start = ((), (), s32[]{:S(2)}) async-start(), calls=%async_computation.1 | async-start | bytes 8847360 | tf_op jit(solution)/shard_map/all_gather | solution.py:59
  8.5 3.5 copy-start.2
  8.7 3.2 collective-permute-start.1
  10.0 5.9 %collective-permute-start = (f32[8,4,24,192]{3,2,0,1:T(8,128)S(1)}, f32[8,4,24,192]{3,2,0,1:T(8,128)S(1)}, u32[]{:S(2)}, u32[]{:S(2)}) collective-permute-start(f32[8,4,24,192]{3,2,0,1:T(8,128)S(1)} %get-tuple-element.10), channel_id=1, source_target_pairs={{16,0},{32,16},{48,32},{64,48},{80,64},{96,80},{112,96},{17,1},{33... | collective-permute-start | bytes 1769480 | tf_op jit(solution)/shard_map/ppermute | solution.py:18
  12.9 3.5 copy-start.1
  16.1 17.1 %copy-start = (f32[8,16,24,192]{3,2,0,1:T(8,128)}, f32[8,16,24,192]{3,2,0,1:T(8,128)S(1)}, u32[]{:S(2)}) copy-start(f32[8,16,24,192]{3,2,0,1:T(8,128)S(1)} %get-tuple-element.12) | copy-start | bytes 7077892
  16.1 17.1 %copy-start.3 = (f32[8,20,24,192]{3,2,0,1:T(8,128)}, f32[8,20,24,192]{3,2,0,1:T(8,128)S(1)}, u32[]{:S(2)}) copy-start(f32[8,20,24,192]{3,2,0,1:T(8,128)S(1)} %get-tuple-element.13) | copy-start | bytes 8847364
  16.4 12.5 %collective-permute-start.2 = (f32[8,20,4,192]{3,2,0,1:T(4,128)S(1)}, f32[8,20,4,192]{3,2,0,1:T(4,128)S(1)}, u32[]{:S(2)}, u32[]{:S(2)}) collective-permute-start(f32[8,20,4,192]{3,2,0,1:T(4,128)S(1)} %get-tuple-element.5), channel_id=1, source_target_pairs={{4,0},{8,4},{12,8},{5,1},{9,5},{13,9},{6,2},{10,6},{14,10},{7,3},{... | collective-permute-start | bytes 1474568 | tf_op jit(solution)/shard_map/ppermute | solution.py:18
  17.7 12.6 %collective-permute-start.3 = (f32[8,20,4,192]{3,2,0,1:T(4,128)S(1)}, f32[8,20,4,192]{3,2,0,1:T(4,128)S(1)}, u32[]{:S(2)}, u32[]{:S(2)}) collective-permute-start(f32[8,20,4,192]{3,2,0,1:T(4,128)S(1)} %get-tuple-element.6), channel_id=1, source_target_pairs={{0,4},{4,8},{8,12},{1,5},{5,9},{9,13},{2,6},{6,10},{10,14},{3,7},{... | collective-permute-start | bytes 1474568 | tf_op jit(solution)/shard_map/ppermute | solution.py:17
  53.9 2.3 copy-start.5
  58.7 311.6 %reduce-scatter.2.cloned.1.call-start = ((), (), s32[]{:S(2)}) async-start(), calls=%async_computation.2 | async-start | bytes 8847360 | tf_op jit(solution)/shard_map/reduce_scatter | solution.py:61
  304.0 66.3 %copy-start.4 = (f32[8,12,4608]{2,0,1:T(8,128)S(1)}, f32[8,12,4608]{2,0,1:T(8,128)}, u32[]{:S(2)}) copy-start(f32[8,12,4608]{2,0,1:T(8,128)} %multiply_add_fusion) | copy-start | bytes 5308420
  304.0 141.3 %all-gather.6.cloned.1.call-start = ((), (), s32[]{:S(2)}) async-start(), calls=%async_computation.3 | async-start | bytes 8847360 | tf_op jit(solution)/shard_map/all_gather | solution.py:65
Sparse Core Ops, SparseCore 0:
  58.8 90.6 all-gather.3
  304.1 66.1 reduce-scatter.1
  373.3 71.9 all-gather.5
